TPU v7x, 256 devices: a whole 4x4x8 slice. The times are simulated.
256 devices in a mesh: obl: 8 (over z_hi, x), scen: 32 (over y, z_lo, core).
Axes of the slice: x: 4, y: 4, z: 8 (z_hi: 2, z_lo: 4; z = z_hi * 4 + z_lo), core: 2. Of those that a mesh axis runs over, the one named last changes fastest.
Arguments:
- loadings: bfloat16 [32768, 256], P('obl', 'scen'), may hold values from -0.375 to 0.375
- scenarios: bfloat16 [256, 131072], P('obl', 'scen'), may hold values from -6 to 6
- rho: float32 [32768], P('obl'), may hold values from 0.05 to 0.5
- exposure: float32 [32768], P('obl'), may hold values from 0.5 to 20
- rating: int32 [32768], P('obl'), may hold values from 0 to 15
- thresholds: float32 [16], replicated, may hold values from -3 to -1
- tail_weight: int32 [131072], P('scen'), may hold values from 1 to 8, as said below
Outputs:
- losses: float32 [131072], P('scen')
- contributions: float32 [32768], P('obl')
- shortfall: float32 [], replicated
Inputs may be any that keep to these rules, and one draw needn't show every extreme that they name: `tail_weight`: weights are larger on average toward later scenarios.
All inputs are finite; a program needn't handle non-finite values.
Results may differ from a plain program's by a relative error of at most 0.0003.
Values may be sent and summed in bfloat16 or wider, within the bound.
A program may use at most 256 MiB of HBM per device.

v0:
```python
import math

import jax
import jax.numpy as jnp
from jax import lax
from jax.sharding import PartitionSpec as P


def normal_cdf(value):
    return 0.5 * lax.erfc(-value * 0.7071067811865476)


def local(loadings, scenarios, rho, exposure, rating, thresholds, tail_weight):
    panel = lax.all_gather(scenarios, "obl", axis=0, tiled=True)
    rows_here = loadings.shape[0]
    cols_here = panel.shape[1]
    width = math.gcd(cols_here, 512)
    nblocks = cols_here // width
    count = rows_here * lax.axis_size("obl")
    buckets = jnp.arange(thresholds.shape[0])
    thr = jnp.sum(
        jnp.where(rating[:, None] == buckets[None, :], thresholds[None, :], jnp.float32(0.0)),
        axis=1,
    )
    root_rho = jnp.sqrt(rho)
    root_rest = jnp.sqrt(1.0 - rho)
    weights = tail_weight.astype(jnp.float32)
    wblocks = weights.reshape(nblocks, width)

    def finish(product, scale, wpart):
        systematic = product * scale[:, None]
        pdef = normal_cdf((thr[:, None] - root_rho[:, None] * systematic) / root_rest[:, None])
        weighted = exposure[:, None] * pdef
        return (jnp.sum(weighted, axis=0) / count, jnp.sum(weighted * wpart[None, :], axis=1))

    full_rows = lax.all_gather(loadings, "scen", axis=1, tiled=True)
    sumsq = jnp.einsum("of,of->o", full_rows, full_rows, preferred_element_type=jnp.float32)
    scale = lax.rsqrt(sumsq + 1e-06)
    panel_blocks = jnp.transpose(panel.reshape(panel.shape[0], nblocks, width), (1, 0, 2))

    def from_panel(pair):
        block, wpart = pair
        product = jnp.dot(full_rows, block, preferred_element_type=jnp.float32)
        return finish(product, scale, wpart)

    loss_blocks, numers = lax.map(from_panel, (panel_blocks, wblocks))
    partial_loss = loss_blocks.reshape(-1)
    numer = jnp.sum(numers, axis=0)
    losses = lax.psum(partial_loss, "obl")
    numer_all, total, tail_loss = lax.psum(
        (numer, jnp.sum(weights), jnp.sum(weights * losses)), "scen"
    )
    contributions = numer_all / total
    shortfall = tail_loss / total
    return (losses, contributions, shortfall)


def solution(mesh):
    placed = (P("obl", "scen"), P("obl", "scen"), P("obl"), P("obl"), P("obl"), P(), P("scen"))
    return jax.shard_map(
        local, mesh=mesh, in_specs=placed, out_specs=(P("scen"), P("obl"), P()), check_vma=False
    )
```

profile of v0, /device:TPU:1, one launch (start us, length us, event | category | flops | bytes accessed | tf_op | source)
XLA Modules:
  0.0 533.3 jit_solution(11336302477741139442)
XLA Ops:
  7.2 0.0 all-gather.3.cloned.1.call-start
  7.2 0.7 all-gather.3.cloned.1.call-update
  7.9 0.0 all-gather.5.cloned.1.call-start
  7.9 0.7 all-gather.5.cloned.1.call-update
  8.7 0.7 convert_element_type.3
  9.4 0.9 select_reduce_fusion
  10.3 0.7 subtract_sqrt_fusion
  11.0 78.3 %all-gather.3.cloned.1.call-done = bf16[256,4096]{1,0:T(8,128)(2,1)} async-done(((bf16[32,4096]{1,0:T(8,128)(2,1)}), bf16[256,4096]{1,0:T(8,128)(2,1)}) %all-gather.3.cloned.1.call-update) | async-done | bytes 2097168 | tf_op jit(solution)/shard_map/all_gather | solution.py:14
  89.3 4.1 copy.17
  93.4 55.2 %all-gather.5.cloned.1.call-done = bf16[4096,256]{0,1:T(8,128)(2,1)} async-done(((bf16[4096,8]{0,1:T(8,128)(2,1)}), bf16[4096,256]{0,1:T(8,128)(2,1)}) %all-gather.5.cloned.1.call-update) | async-done | bytes 2097168 | tf_op jit(solution)/shard_map/all_gather | solution.py:36
  148.6 0.0 copy-start
  148.6 2.2 fusion.19
  150.8 0.0 copy-done
  150.9 0.0 copy-start.1
  150.9 2.5 copy.19
  153.3 0.0 copy-done.1
  153.3 0.0 copy-start.2
  153.3 188.8 %while.12 = (s32[]{:T(128)}, f32[8,512]{1,0:T(8,128)S(1)}, f32[8,4096]{1,0:T(8,128)S(1)}, f32[4096]{0:T(1024)S(1)}, f32[4096]{0:T(1024)S(1)}, /*index=5*/bf16[8,...) while((s32[]{:T(128)}, f32[8,512]{1,0:T(8,128)S(1)}, ...), condition=%wide.region_4.5_spmd, body=%wide.region_1.4_spmd.sunk | while | flops 1220542464 | bytes 2539669 | solution.py:46
  153.4 23.1 %multiply_reduce_fusion.3 = (f32[4096]{0:T(1024)S(1)}, f32[512]{0:T(512)S(1)}) fusion(f32[512]{0:T(512)S(1)} %bitcast.86, f32[4096]{0:T(1024)S(1)} %broadcast_multiply_fusion.4, f32[4096]{0:T(1024)S(1)} %get-tuple-element.232, f32[4096]{0:T(1024)S(1)} %get-tuple-element.231, bf16[4096,256]{1,0:T(8,128)(2,1)} %get-tuple-element.230, ...), kind=kOutput, calls=%fused_computation.9.clone.1 | convolution fusion | flops 1220537856 | bytes 2461700 | tf_op jit(solution)/shard_map/while/body/eval_jaxpr/dot_general | solution.py:43
  176.5 0.1 dynamic_update_slice.10
  176.5 0.4 dynamic_update_slice.11
  177.0 23.1 %multiply_reduce_fusion.3 = (f32[4096]{0:T(1024)S(1)}, f32[512]{0:T(512)S(1)}) fusion(f32[512]{0:T(512)S(1)} %bitcast.86, f32[4096]{0:T(1024)S(1)} %broadcast_multiply_fusion.4, f32[4096]{0:T(1024)S(1)} %get-tuple-element.232, f32[4096]{0:T(1024)S(1)} %get-tuple-element.231, bf16[4096,256]{1,0:T(8,128)(2,1)} %get-tuple-element.230, ...), kind=kOutput, calls=%fused_computation.9.clone.1 | convolution fusion | flops 1220537856 | bytes 2461700 | tf_op jit(solution)/shard_map/while/body/eval_jaxpr/dot_general | solution.py:43
  200.1 0.1 dynamic_update_slice.10
  200.1 0.4 dynamic_update_slice.11
  200.6 23.1 %multiply_reduce_fusion.3 = (f32[4096]{0:T(1024)S(1)}, f32[512]{0:T(512)S(1)}) fusion(f32[512]{0:T(512)S(1)} %bitcast.86, f32[4096]{0:T(1024)S(1)} %broadcast_multiply_fusion.4, f32[4096]{0:T(1024)S(1)} %get-tuple-element.232, f32[4096]{0:T(1024)S(1)} %get-tuple-element.231, bf16[4096,256]{1,0:T(8,128)(2,1)} %get-tuple-element.230, ...), kind=kOutput, calls=%fused_computation.9.clone.1 | convolution fusion | flops 1220537856 | bytes 2461700 | tf_op jit(solution)/shard_map/while/body/eval_jaxpr/dot_general | solution.py:43
  223.7 0.1 dynamic_update_slice.10
  223.7 0.4 dynamic_update_slice.11
  224.2 23.1 %multiply_reduce_fusion.3 = (f32[4096]{0:T(1024)S(1)}, f32[512]{0:T(512)S(1)}) fusion(f32[512]{0:T(512)S(1)} %bitcast.86, f32[4096]{0:T(1024)S(1)} %broadcast_multiply_fusion.4, f32[4096]{0:T(1024)S(1)} %get-tuple-element.232, f32[4096]{0:T(1024)S(1)} %get-tuple-element.231, bf16[4096,256]{1,0:T(8,128)(2,1)} %get-tuple-element.230, ...), kind=kOutput, calls=%fused_computation.9.clone.1 | convolution fusion | flops 1220537856 | bytes 2461700 | tf_op jit(solution)/shard_map/while/body/eval_jaxpr/dot_general | solution.py:43
  247.2 0.1 dynamic_update_slice.10
  247.3 0.4 dynamic_update_slice.11
  247.8 23.1 %multiply_reduce_fusion.3 = (f32[4096]{0:T(1024)S(1)}, f32[512]{0:T(512)S(1)}) fusion(f32[512]{0:T(512)S(1)} %bitcast.86, f32[4096]{0:T(1024)S(1)} %broadcast_multiply_fusion.4, f32[4096]{0:T(1024)S(1)} %get-tuple-element.232, f32[4096]{0:T(1024)S(1)} %get-tuple-element.231, bf16[4096,256]{1,0:T(8,128)(2,1)} %get-tuple-element.230, ...), kind=kOutput, calls=%fused_computation.9.clone.1 | convolution fusion | flops 1220537856 | bytes 2461700 | tf_op jit(solution)/shard_map/while/body/eval_jaxpr/dot_general | solution.py:43
  270.8 0.1 dynamic_update_slice.10
  270.9 0.4 dynamic_update_slice.11
  271.4 23.1 %multiply_reduce_fusion.3 = (f32[4096]{0:T(1024)S(1)}, f32[512]{0:T(512)S(1)}) fusion(f32[512]{0:T(512)S(1)} %bitcast.86, f32[4096]{0:T(1024)S(1)} %broadcast_multiply_fusion.4, f32[4096]{0:T(1024)S(1)} %get-tuple-element.232, f32[4096]{0:T(1024)S(1)} %get-tuple-element.231, bf16[4096,256]{1,0:T(8,128)(2,1)} %get-tuple-element.230, ...), kind=kOutput, calls=%fused_computation.9.clone.1 | convolution fusion | flops 1220537856 | bytes 2461700 | tf_op jit(solution)/shard_map/while/body/eval_jaxpr/dot_general | solution.py:43
  294.4 0.1 dynamic_update_slice.10
  294.5 0.4 dynamic_update_slice.11
  294.9 23.1 %multiply_reduce_fusion.3 = (f32[4096]{0:T(1024)S(1)}, f32[512]{0:T(512)S(1)}) fusion(f32[512]{0:T(512)S(1)} %bitcast.86, f32[4096]{0:T(1024)S(1)} %broadcast_multiply_fusion.4, f32[4096]{0:T(1024)S(1)} %get-tuple-element.232, f32[4096]{0:T(1024)S(1)} %get-tuple-element.231, bf16[4096,256]{1,0:T(8,128)(2,1)} %get-tuple-element.230, ...), kind=kOutput, calls=%fused_computation.9.clone.1 | convolution fusion | flops 1220537856 | bytes 2461700 | tf_op jit(solution)/shard_map/while/body/eval_jaxpr/dot_general | solution.py:43
  318.0 0.1 dynamic_update_slice.10
  318.1 0.4 dynamic_update_slice.11
  318.5 23.1 %multiply_reduce_fusion.3 = (f32[4096]{0:T(1024)S(1)}, f32[512]{0:T(512)S(1)}) fusion(f32[512]{0:T(512)S(1)} %bitcast.86, f32[4096]{0:T(1024)S(1)} %broadcast_multiply_fusion.4, f32[4096]{0:T(1024)S(1)} %get-tuple-element.232, f32[4096]{0:T(1024)S(1)} %get-tuple-element.231, bf16[4096,256]{1,0:T(8,128)(2,1)} %get-tuple-element.230, ...), kind=kOutput, calls=%fused_computation.9.clone.1 | convolution fusion | flops 1220537856 | bytes 2461700 | tf_op jit(solution)/shard_map/while/body/eval_jaxpr/dot_general | solution.py:43
  341.6 0.1 dynamic_update_slice.10
  341.7 0.4 dynamic_update_slice.11
  342.1 45.3 %psum.28 = f32[4096]{0:T(1024)S(1)} all-reduce(f32[4096]{0:T(1024)S(1)} %bitcast.85), channel_id=1, replica_groups=mesh['obl'=8,'scen'=32] {'obl'}, use_global_device_ids=true, to_apply=%region_5.6 | all-reduce | flops 4096 | bytes 32768 | tf_op jit(solution)/shard_map/psum | solution.py:49
  387.4 0.0 copy-done.2
  387.4 0.6 multiply_reduce_fusion.1
  388.1 134.6 %all-reduce = (f32[4096]{0:T(1024)S(1)}, f32[]{:T(128)}, f32[]{:T(128)}) all-reduce(f32[4096]{0:T(1024)S(1)} %reduce_sum.55, f32[]{:T(128)} %get-tuple-element.99, f32[]{:T(128)} %get-tuple-element.98), channel_id=1, replica_groups=mesh['obl'=8,'scen'=32] {'scen'}, use_global_device_ids=true, to_apply=%region_7.8 | all-reduce | flops 4098 | bytes 32784 | tf_op jit(solution)/shard_map/psum | solution.py:50
  524.1 1.3 broadcast_divide_fusion
  525.4 0.0 copy-done.3
  (31 shorter events, 0.2 us)
Async XLA Ops:
  7.2 82.2 %all-gather.3.cloned.1.call-start = ((), (), s32[]{:S(2)}) async-start(), calls=%async_computation | async-start | bytes 2359296 | tf_op jit(solution)/shard_map/all_gather | solution.py:14
  7.9 140.7 %all-gather.5.cloned.1.call-start = ((), (), s32[]{:S(2)}) async-start(), calls=%async_computation.1 | async-start | bytes 2162688 | tf_op jit(solution)/shard_map/all_gather | solution.py:36
  148.6 2.2 copy-start
  150.9 2.5 copy-start.1
  153.3 234.1 %copy-start.2 = (s32[4096]{0:T(1024)S(1)}, s32[4096]{0:T(1024)}, u32[]{:S(2)}) copy-start(s32[4096]{0:T(1024)} %param.15) | copy-start | bytes 49156
  387.4 137.9 %copy-start.3 = (f32[4096]{0:T(1024)}, f32[4096]{0:T(1024)S(1)}, u32[]{:S(2)}) copy-start(f32[4096]{0:T(1024)S(1)} %psum.28) | copy-start | bytes 49156
Sparse Core Ops, SparseCore 0:
  10.6 78.6 all-gather.2
  91.2 57.4 all-gather.4
where the time goes:
time: 537 us; the launch traced here: 533 us
  matrix products  185 us (34%)
  blocking collectives  180 us (34%)
  waiting for transfers between devices  135 us (25%)
  between operations  16.6 us (3%)
  local copies, waits for them, and re-layouts  10.3 us (2%)
  other arithmetic  6.52 us (1%)
    dot_general x8, matrix products, from_panel(): product = jnp.dot(full_rows, block, preferred_element_type=jnp.float32)  185 us
    psum x1, blocking collectives, local(): lax.psum((numer, jnp.sum(weights), jnp.sum(weights * losses)), 'scen')  135 us
    all_gather x1, waiting for transfers between devices, local(): panel = lax.all_gather(scenarios, 'obl', axis=0, tiled=True)  78.3 us
    all_gather x1, waiting for transfers between devices, local(): full_rows = lax.all_gather(loadings, 'scen', axis=1, tiled=True)  55.2 us
    psum x1, blocking collectives, local(): losses = lax.psum(partial_loss, 'obl')  45.3 us
  transfers between devices with their start and end apart: 2, of which 2 were waited for; matrix products, arithmetic and copies ran while one was open for 1% of the time, Pallas kernels for 0%

commit v1 on v0

v1 whole, which is shorter than its diff:
```python
import functools

import jax
import jax.numpy as jnp
import numpy as np
from jax import lax
from jax.experimental import pallas as pl
from jax.experimental.pallas import tpu as pltpu
from jax.sharding import PartitionSpec as P

LANES = 128
ROWS = 256
COLS = 512

SCALE = float(2.0**-3.4)
OFFSET = float(5.2 * 2.0**-3.4)
COEFFS = (
    -24.48703166417573,
    -58.39165125696405,
    -57.73044940308441,
    -31.529938430810628,
    -11.50559434722367,
    -3.36061823149743,
    -0.771910203459282,
    -0.15406865262823627,
    -0.033933149049334255,
)


def scenario_losses(
    thresholds, lt_ref, s_ref, rho, exposure, rating, weight, loss_out, cont_out,
    st, wide_weight, loss, cont, shift, slope, expo, base, prod_a, prod_b,
):
    factors, nobl = lt_ref.shape
    nsc = s_ref.shape[1]

    for r in range(nobl // LANES):
        block = lt_ref[:, r * LANES : (r + 1) * LANES].astype(jnp.float32)
        slope[r : r + 1, :] = jnp.sum(block * block, axis=0, keepdims=True)
    kind = rating[...]
    thr = jnp.zeros(kind.shape, jnp.float32)
    for k in range(thresholds.shape[0]):
        thr = jnp.where(kind == k, thresholds[k], thr)
    root_rest = jnp.sqrt(1.0 - rho[...])
    scale = lax.rsqrt(slope[...] + 1e-06)
    shift[...] = thr / root_rest * SCALE
    slope[...] = -(jnp.sqrt(rho[...]) * scale / root_rest) * SCALE
    expo[...] = exposure[...]
    base[...] = jnp.log2(exposure[...]) + COEFFS[0]

    @pl.loop(0, nsc // LANES)
    def _(r):
        at = pl.ds(pl.multiple_of(r * LANES, LANES), LANES)
        st[at, :] = s_ref[:, at].T
        row = weight[pl.ds(r, 1), :].astype(jnp.float32)
        wide_weight[at, :] = jnp.broadcast_to(row, (LANES, LANES)).T

    loss[...] = jnp.zeros_like(loss)
    cont[...] = jnp.zeros_like(cont)
    per = nsc // ROWS
    steps = per * (nobl // COLS)

    def product(step, into):
        jb, ib = step // per, step % per
        rows = pl.ds(pl.multiple_of(ib * ROWS, ROWS), ROWS)
        cols = pl.ds(pl.multiple_of(jb * COLS, COLS), COLS)
        into[...] = jnp.dot(st[rows, :], lt_ref[:, cols], preferred_element_type=jnp.float32)

    tiles = COLS // LANES

    def spread(ref, jb):
        return [jnp.broadcast_to(ref[pl.ds(jb * tiles + j, 1), :], (8, LANES)) for j in range(tiles)]

    def reduce_step(step, prod):
        jb, ib = step // per, step % per
        a, b, e, g = spread(shift, jb), spread(slope, jb), spread(expo, jb), spread(base, jb)
        total = [jnp.zeros((8, LANES), jnp.float32) for _ in range(tiles)]
        for r in range(ROWS // 8):
            at = pl.ds(pl.multiple_of(ib * ROWS + r * 8, 8), 8)
            w = wide_weight[at, :]
            partial = None
            for j in range(tiles):
                v = prod[r * 8 : r * 8 + 8, j * LANES : (j + 1) * LANES] * b[j] + a[j]
                y = jnp.log2(jnp.abs(v) + OFFSET)
                q = y * COEFFS[-1] + COEFFS[-2]
                for c in COEFFS[-3:0:-1]:
                    q = q * y + c
                tail = jnp.exp2(q * y + g[j])
                x = jnp.where(v < 0.0, tail, e[j] - tail)
                total[j] = total[j] + x * w
                partial = x if partial is None else partial + x
            loss[at, :] = loss[at, :] + partial
        for j in range(tiles):
            at = pl.ds(pl.multiple_of(jb * COLS + j * LANES, LANES), LANES)
            cont[:, at] = cont[:, at] + total[j]

    product(0, prod_a)

    @pl.loop(0, steps // 2)
    def _(k):
        product(2 * k + 1, prod_b)
        reduce_step(2 * k, prod_a)
        product(jnp.minimum(2 * k + 2, steps - 1), prod_a)
        reduce_step(2 * k + 1, prod_b)

    for r in range(nsc // LANES):
        loss_out[r : r + 1, :] = jnp.sum(loss[r * LANES : (r + 1) * LANES, :].T, axis=0, keepdims=True)
    for r in range(nobl // LANES):
        cont_out[r : r + 1, :] = jnp.sum(cont[:, r * LANES : (r + 1) * LANES], axis=0, keepdims=True)


def compute(lt, s, rho, exposure, rating, thresholds, weight):
    factors, nobl = lt.shape
    nsc = s.shape[1]
    rows, cols = nobl // LANES, nsc // LANES
    vmem = pl.BlockSpec(memory_space=pltpu.VMEM)
    f32 = jnp.float32
    return pl.pallas_call(
        scenario_losses,
        name="scenario_losses",
        out_shape=(
            jax.ShapeDtypeStruct((cols, LANES), f32),
            jax.ShapeDtypeStruct((rows, LANES), f32),
        ),
        in_specs=[pl.BlockSpec(memory_space=pltpu.SMEM)] + [vmem] * 6,
        out_specs=(vmem, vmem),
        scratch_shapes=[
            pltpu.VMEM((nsc, factors), jnp.bfloat16),
            pltpu.VMEM((nsc, LANES), f32),
            pltpu.VMEM((nsc, LANES), f32),
            pltpu.VMEM((8, nobl), f32),
            pltpu.VMEM((rows, LANES), f32),
            pltpu.VMEM((rows, LANES), f32),
            pltpu.VMEM((rows, LANES), f32),
            pltpu.VMEM((rows, LANES), f32),
            pltpu.VMEM((ROWS, COLS), f32),
            pltpu.VMEM((ROWS, COLS), f32),
        ],
    )(
        thresholds, lt, s, rho.reshape(rows, LANES), exposure.reshape(rows, LANES),
        rating.reshape(rows, LANES), weight.reshape(cols, LANES),
    )


def local(loadings, scenarios, rho, exposure, rating, thresholds, tail_weight):
    panel = lax.all_gather(scenarios, "obl", axis=0, tiled=True)
    lt = lax.all_gather(loadings.T, "scen", axis=0, tiled=True)
    count = loadings.shape[0] * lax.axis_size("obl")
    loss, cont = compute(lt, panel, rho, exposure, rating, thresholds, tail_weight)
    weights = tail_weight.astype(jnp.float32)
    losses = lax.psum(loss.reshape(-1), "obl") / count
    numer, total = lax.psum((cont.reshape(-1), jnp.sum(weights)), "scen")
    contributions = numer / total
    shortfall = lax.psum(jnp.sum(contributions), "obl") / count
    return (losses, contributions, shortfall)


def solution(mesh):
    placed = (P("obl", "scen"), P("obl", "scen"), P("obl"), P("obl"), P("obl"), P(), P("scen"))
    return jax.shard_map(
        local, mesh=mesh, in_specs=placed, out_specs=(P("scen"), P("obl"), P()), check_vma=False
    )
```

time: 537 us -> 429 us (0.80)
  the two profiles are of different devices: /device:TPU:1 before, /device:TPU:0 now
where the time goes in v1:
time: 429 us; the launch traced here: 428 us
  blocking collectives  190 us (44%)
  waiting for transfers between devices  137 us (32%)
  Pallas kernels  81.9 us (19%)
  between operations  15.8 us (4%)
    psum x1, blocking collectives, local(): numer, total = lax.psum((cont.reshape(-1), jnp.sum(weights)), 'scen')  136 us
    pallas_call x1, Pallas kernels, compute(): pl.pallas_call(scenario_losses, name='scenario_losses', out_shape=(jax.Sh...  81.9 us
    all_gather x1, waiting for transfers between devices, local(): panel = lax.all_gather(scenarios, 'obl', axis=0, tiled=True)  78.1 us
    all_gather x1, waiting for transfers between devices, local(): lt = lax.all_gather(loadings.T, 'scen', axis=0, tiled=True)  57.6 us
    psum x1, blocking collectives, local(): losses = lax.psum(loss.reshape(-1), 'obl') / count  53.7 us
  transfers between devices with their start and end apart: 2, of which 2 were waited for; matrix products, arithmetic and copies ran while one was open for 0% of the time, Pallas kernels for 0%

profile of v1, /device:TPU:0, one launch (start us, length us, event | category | flops | bytes accessed | tf_op | source)
XLA Modules:
  0.0 428.4 jit_solution(2283534733730775593)
XLA Ops:
  7.2 0.0 all-gather.5.cloned.1.call-start
  7.2 0.7 all-gather.5.cloned.1.call-update
  7.9 0.0 all-gather.3.cloned.1.call-start
  7.9 0.7 all-gather.3.cloned.1.call-update
  8.6 1.3 convert_reduce_fusion
  10.0 78.1 %all-gather.5.cloned.1.call-done.s_ref = bf16[256,4096]{1,0:T(8,128)(2,1)} async-done(((bf16[32,4096]{1,0:T(8,128)(2,1)}), bf16[256,4096]{1,0:T(8,128)(2,1)}) %all-gather.5.cloned.1.call-update) | async-done | bytes 2097168 | tf_op jit(solution)/shard_map/all_gather | solution.py:146
  88.1 57.6 %all-gather.3.cloned.1.call-done.lt_ref = bf16[256,4096]{1,0:T(8,128)(2,1)} async-done(((bf16[8,4096]{1,0:T(8,128)(2,1)}), bf16[256,4096]{1,0:T(8,128)(2,1)}) %all-gather.3.cloned.1.call-update) | async-done | bytes 2097168 | tf_op jit(solution)/shard_map/all_gather | solution.py:147
  145.7 81.9 %scenario_losses.1 = (f32[32,128]{1,0:T(8,128)}, f32[32,128]{1,0:T(8,128)}) custom-call(f32[16]{0:T(128)} %thresholds.1, bf16[256,4096]{1,0:T(8,128)(2,1)} %all-gather.3.cloned.1.call-done.lt_ref, bf16[256,4096]{1,0:T(8,128)(2,1)} %all-gather.5.cloned.1.call-done.s_ref, f32[32,128]{1,0:T(8,128)} %bitcast.9, f32[32,128]{1,0:T(8,128)} %bitcast.10, ...), custom_call_target="tpu_custom_call" | custom-call | tf_op jit(solution)/shard_map/scenario_losses/pallas_call | solution.py:118
  227.6 136.0 %all-reduce = (f32[4096]{0:T(1024)S(1)}, f32[]{:T(128)}) all-reduce(f32[4096]{0:T(1024)} %bitcast.13, f32[]{:T(128)} %convert_reduce_fusion), channel_id=1, replica_groups=mesh['obl'=8,'scen'=32] {'scen'}, use_global_device_ids=true, to_apply=%region_1.0 | all-reduce | flops 4097 | bytes 32776 | tf_op jit(solution)/shard_map/psum | solution.py:152
  363.5 1.9 fusion
  365.5 53.7 %all-reduce.1 = (f32[4096]{0:T(1024)S(1)}, f32[]{:T(128)}) all-reduce(f32[4096]{0:T(1024)} %bitcast.12, f32[]{:T(128)} %get-tuple-element.11), channel_id=1, replica_groups=mesh['obl'=8,'scen'=32] {'obl'}, use_global_device_ids=true, to_apply=%region_0.0 | all-reduce | flops 4097 | bytes 32776 | tf_op jit(solution)/shard_map/psum | solution.py:151
  419.2 0.6 broadcast_multiply_fusion
Async XLA Ops:
  7.2 80.9 %all-gather.5.cloned.1.call-start = ((), (), s32[]{:S(2)}) async-start(), calls=%async_computation.1 | async-start | bytes 2359296 | tf_op jit(solution)/shard_map/all_gather | solution.py:146
  7.9 137.8 %all-gather.3.cloned.1.call-start = ((), (), s32[]{:S(2)}) async-start(), calls=%async_computation | async-start | bytes 2162688 | tf_op jit(solution)/shard_map/all_gather | solution.py:147
Sparse Core Ops, SparseCore 0:
  10.6 77.3 all-gather.4
  89.9 55.7 all-gather.2

commit v2 on v1

--- a/solution.py
+++ b/solution.py
@@ -27,16 +27,230 @@
 )
 
 
+MESH = pl.DeviceIdType.MESH
+X, Z, Y, CORES = 4, 4, 4, 2
+TILE = 8
+
+
+def place():
+    obl, scen = lax.axis_index("obl"), lax.axis_index("scen")
+    return obl // X, obl % X, scen // (Z * CORES), scen // CORES % Z, scen % CORES
+
+
+def obl_at(far, x):
+    return far * X + x
+
+
+def scen_at(y, z, core):
+    return (y * Z + z) * CORES + core
+
+
+class Links:
+    def __init__(self, send_sems):
+        self.sems, self.started = send_sems, []
+
+    def send(self, source, target, recv_sem, obl, scen):
+        copy = pltpu.make_async_remote_copy(
+            src_ref=source, dst_ref=target, send_sem=self.sems.at[len(self.started)],
+            recv_sem=recv_sem, device_id={"obl": obl, "scen": scen}, device_id_type=MESH,
+        )
+        copy.start()
+        self.started.append(copy)
+
+    def receive(self, target, recv_sem):
+        pltpu.make_async_remote_copy(
+            src_ref=target, dst_ref=target, send_sem=self.sems.at[0], recv_sem=recv_sem,
+            device_id={"obl": lax.axis_index("obl"), "scen": lax.axis_index("scen")},
+            device_id_type=MESH,
+        ).wait_recv()
+
+    def finish(self):
+        for copy in self.started:
+            copy.wait_send()
+
+
+GATHER_SENDS = 9 + 3 + 16 + 16
+REDUCE_SENDS = 2 + 3 + 3 + 3 + 31
+
+
+def meet(peers):
+    barrier = pltpu.get_barrier_semaphore()
+    for obl, scen in peers:
+        pl.semaphore_signal(
+            barrier, inc=1, device_id={"obl": obl, "scen": scen}, device_id_type=MESH)
+    pl.semaphore_wait(barrier, len(peers))
+
+
+def gather(loads, scenarios, lt3, panel, send_sems, local_sem, panel_sem, loads_sem):
+    far, x, y, z, core = place()
+    obl, scen = lax.axis_index("obl"), lax.axis_index("scen")
+    height, nsc = scenarios.shape
+    nobl = loads.shape[1]
+    half_h, half_w = height // 2, nobl // 2
+    right, left = (x + 1) % X, (x + X - 1) % X
+    up, down = (y + 1) % Y, (y + Y - 1) % Y
+    meet(
+        [(obl_at(1 - far, x), scen), (obl_at(far, left), scen), (obl_at(far, right), scen)]
+        + [(obl, scen_at(to, z, core)) for to in (up, down)]
+        + [(obl, scen_at(y, (z + k) % Z, core)) for k in range(1, Z)]
+        + [(obl, scen_at(y, z, 1 - core))]
+    )
+    links = Links(send_sems)
+
+    def rows(owner, start=0, size=height):
+        return panel.at[pl.ds(pl.multiple_of(owner * height + start, half_h), size), :]
+
+    own_rows = pltpu.make_async_copy(scenarios, rows(obl), local_sem.at[0])
+    own_loads = pltpu.make_async_copy(loads, lt3.at[scen], local_sem.at[1])
+    own_rows.start()
+    own_loads.start()
+
+    def panel_out(source, owner):
+        for to in (right, left):
+            links.send(source, rows(owner), panel_sem.at[owner, 0], obl_at(far, to), scen)
+
+    def panel_relay(row):
+        low, high = obl_at(row, left), obl_at(row, right)
+        links.receive(rows(low), panel_sem.at[low, 0])
+        links.send(
+            rows(low, 0, half_h), rows(low, 0, half_h), panel_sem.at[low, 0], obl_at(far, right), scen)
+        links.receive(rows(high), panel_sem.at[high, 0])
+        links.send(
+            rows(high, half_h, half_h), rows(high, half_h, half_h), panel_sem.at[high, 1],
+            obl_at(far, left), scen)
+
+    def panel_last(row):
+        across = obl_at(row, (x + 2) % X)
+        links.receive(rows(across, 0, half_h), panel_sem.at[across, 0])
+        links.receive(rows(across, half_h, half_h), panel_sem.at[across, 1])
+
+    def strip(owner, part=None):
+        if part is None:
+            return lt3.at[owner]
+        return lt3.at[owner, :, pl.ds(part * half_w, half_w)]
+
+    def loads_out(source, owner):
+        for to in (up, down):
+            links.send(source, strip(owner), loads_sem.at[owner, 0], obl, scen_at(to, z, core))
+        loads_across(source, owner)
+
+    def loads_across(source, owner):
+        links.send(source, strip(owner), loads_sem.at[owner, 0], obl, scen_at(y, z, 1 - core))
+
+    def loads_relay(run):
+        low, high = scen_at(down, run, core), scen_at(up, run, core)
+        links.receive(strip(low), loads_sem.at[low, 0])
+        links.send(strip(low, 0), strip(low, 0), loads_sem.at[low, 0], obl, scen_at(up, z, core))
+        loads_across(strip(low), low)
+        links.receive(strip(high), loads_sem.at[high, 0])
+        links.send(strip(high, 1), strip(high, 1), loads_sem.at[high, 1], obl, scen_at(down, z, core))
+        loads_across(strip(high), high)
+
+    def loads_last(run):
+        opposite = scen_at((y + 2) % Y, run, core)
+        links.receive(strip(opposite, 0), loads_sem.at[opposite, 0])
+        links.receive(strip(opposite, 1), loads_sem.at[opposite, 1])
+        loads_across(strip(opposite), opposite)
+
+    runs = [(z + k) % Z for k in range(Z)]
+    for run in runs[1:]:
+        links.send(loads, strip(scen), loads_sem.at[scen, 0], obl, scen_at(y, run, core))
+    links.send(scenarios, rows(obl), panel_sem.at[obl, 0], obl_at(1 - far, x), scen)
+    panel_out(scenarios, obl)
+    loads_out(loads, scen)
+    for run in runs[1:]:
+        owner = scen_at(y, run, core)
+        links.receive(strip(owner), loads_sem.at[owner, 0])
+        loads_out(strip(owner), owner)
+    loads_relay(runs[0])
+    panel_relay(far)
+    other = obl_at(1 - far, x)
+    links.receive(rows(other), panel_sem.at[other, 0])
+    panel_out(rows(other), other)
+    for run in runs[1:]:
+        loads_relay(run)
+    for run in runs:
+        loads_last(run)
+    panel_relay(1 - far)
+    for run in range(Z):
+        for k in range(Y):
+            owner = scen_at(k, run, 1 - core)
+            links.receive(strip(owner), loads_sem.at[owner, 0])
+    own_rows.wait()
+    own_loads.wait()
+    panel_last(far)
+    panel_last(1 - far)
+    links.finish()
+
+
+def reduce(
+    count, loss_a, cont_a, weight, losses_out, cont_out, short_out,
+    loss_z, loss_x, cont_c, cont_z, cont_y, tiles,
+    send_sems, sums_sem, loss_sem, run_sem, y_sem, tile_sem,
+):
+    far, x, y, z, core = place()
+    obl, scen = lax.axis_index("obl"), lax.axis_index("scen")
+    nrows = losses_out.shape[0]
+    group = Y * Z * CORES
+    meet(
+        [(obl_at(1 - far, x), scen)]
+        + [(obl_at(far, (x + k) % X), scen) for k in range(1, X)]
+        + [(obl, (scen + k) % group) for k in range(1, group)]
+    )
+    links = Links(send_sems)
+    weights = weight[...].astype(jnp.float32)
+    weight_sum = jnp.sum(jnp.sum(weights, axis=0, keepdims=True), axis=1, keepdims=True)
+
+    links.send(loss_a, loss_z, sums_sem.at[0], obl_at(1 - far, x), scen)
+    links.send(cont_a, cont_c, sums_sem.at[1], obl, scen_at(y, z, 1 - core))
+    links.receive(cont_c, sums_sem.at[1])
+    cont_z[z] = cont_a[...] + cont_c[...]
+    for k in range(1, Z):
+        links.send(cont_z.at[z], cont_z.at[z], run_sem.at[z], obl, scen_at(y, (z + k) % Z, core))
+    links.receive(loss_z, sums_sem.at[0])
+    loss_x[x] = loss_a[...] + loss_z[...]
+    for k in range(1, X):
+        links.send(loss_x.at[x], loss_x.at[x], loss_sem.at[x], obl_at(far, (x + k) % X), scen)
+    for k in range(1, Z):
+        links.receive(cont_z.at[(z + k) % Z], run_sem.at[(z + k) % Z])
+    cont_y[y] = cont_z[0] + cont_z[1] + cont_z[2] + cont_z[3]
+    for k in range(1, Y):
+        links.send(cont_y.at[y], cont_y.at[y], y_sem.at[y], obl, scen_at((y + k) % Y, z, core))
+    for k in range(1, X):
+        links.receive(loss_x.at[(x + k) % X], loss_sem.at[(x + k) % X])
+    whole = loss_x[0] + loss_x[1] + loss_x[2] + loss_x[3]
+    losses_out[...] = whole[:nrows] / count
+    upper = lax.broadcasted_iota(jnp.int32, (TILE, LANES), 0) < TILE // 2
+    tiles[scen] = jnp.where(upper, whole[nrows:], jnp.broadcast_to(weight_sum, (TILE, LANES)))
+    for k in range(1, group):
+        links.send(tiles.at[scen], tiles.at[scen], tile_sem.at[scen], obl, (scen + k) % group)
+    for k in range(1, Y):
+        links.receive(cont_y.at[(y + k) % Y], y_sem.at[(y + k) % Y])
+    numer = cont_y[0] + cont_y[1] + cont_y[2] + cont_y[3]
+    for k in range(1, group):
+        links.receive(tiles.at[(scen + k) % group], tile_sem.at[(scen + k) % group])
+    scalars = jnp.sum(tiles[...], axis=0)
+    total = scalars[TILE - 1 : TILE, :]
+    cont_out[...] = numer / total
+    short_out[...] = jnp.broadcast_to(scalars[0:1, :] / total / count, (TILE, LANES))
+    links.finish()
+
+
 def scenario_losses(
-    thresholds, lt_ref, s_ref, rho, exposure, rating, weight, loss_out, cont_out,
-    st, wide_weight, loss, cont, shift, slope, expo, base, prod_a, prod_b,
+    thresholds, lt3, panel, rho, exposure, rating, weight, loss_out, cont_out,
+    lt, st, wide_weight, loss, cont, shift, slope, expo, base, prod_a, prod_b,
 ):
-    factors, nobl = lt_ref.shape
-    nsc = s_ref.shape[1]
+    factors, nobl = lt.shape
+    nsc = panel.shape[1]
 
     for r in range(nobl // LANES):
-        block = lt_ref[:, r * LANES : (r + 1) * LANES].astype(jnp.float32)
-        slope[r : r + 1, :] = jnp.sum(block * block, axis=0, keepdims=True)
+        at = slice(r * LANES, (r + 1) * LANES)
+        square = jnp.zeros((TILE, LANES), jnp.float32)
+        for k in range(0, factors // TILE, 2):
+            one, two = lt3[k, :, at].astype(jnp.float32), lt3[k + 1, :, at].astype(jnp.float32)
+            square = square + one * one + two * two
+            lt[k * TILE : (k + 2) * TILE, at] = jnp.concatenate([one, two], axis=0).astype(jnp.bfloat16)
+        slope[r : r + 1, :] = jnp.sum(square, axis=0, keepdims=True)
     kind = rating[...]
     thr = jnp.zeros(kind.shape, jnp.float32)
     for k in range(thresholds.shape[0]):
@@ -51,7 +265,7 @@
     @pl.loop(0, nsc // LANES)
     def _(r):
         at = pl.ds(pl.multiple_of(r * LANES, LANES), LANES)
-        st[at, :] = s_ref[:, at].T
+        st[at, :] = panel[:, at].T
         row = weight[pl.ds(r, 1), :].astype(jnp.float32)
         wide_weight[at, :] = jnp.broadcast_to(row, (LANES, LANES)).T
 
@@ -64,7 +278,7 @@
         jb, ib = step // per, step % per
         rows = pl.ds(pl.multiple_of(ib * ROWS, ROWS), ROWS)
         cols = pl.ds(pl.multiple_of(jb * COLS, COLS), COLS)
-        into[...] = jnp.dot(st[rows, :], lt_ref[:, cols], preferred_element_type=jnp.float32)
+        into[...] = jnp.dot(st[rows, :], lt[:, cols], preferred_element_type=jnp.float32)
 
     tiles = COLS // LANES
 
@@ -107,52 +321,73 @@
         loss_out[r : r + 1, :] = jnp.sum(loss[r * LANES : (r + 1) * LANES, :].T, axis=0, keepdims=True)
     for r in range(nobl // LANES):
         cont_out[r : r + 1, :] = jnp.sum(cont[:, r * LANES : (r + 1) * LANES], axis=0, keepdims=True)
-
-
-def compute(lt, s, rho, exposure, rating, thresholds, weight):
-    factors, nobl = lt.shape
-    nsc = s.shape[1]
+    numer_here = jnp.sum(jnp.sum(cont_out[...], axis=0, keepdims=True), axis=1, keepdims=True)
+    loss_out[nsc // LANES :, :] = jnp.broadcast_to(numer_here, (TILE, LANES))
+
+
+def local(loadings, scenarios, rho, exposure, rating, thresholds, tail_weight):
+    nobl, nsc = loadings.shape[0], scenarios.shape[1]
+    far_x, group = lax.axis_size("obl"), lax.axis_size("scen")
+    factors = scenarios.shape[0] * far_x
+    count = nobl * far_x
     rows, cols = nobl // LANES, nsc // LANES
     vmem = pl.BlockSpec(memory_space=pltpu.VMEM)
-    f32 = jnp.float32
-    return pl.pallas_call(
+    f32, bf16, dma = jnp.float32, jnp.bfloat16, pltpu.SemaphoreType.DMA
+    weight = tail_weight.reshape(cols, LANES)
+
+    def wide(*shape):
+        return pltpu.VMEM(shape, f32)
+
+    lt3, panel = pl.pallas_call(
+        gather,
+        name="gather",
+        out_shape=(
+            jax.ShapeDtypeStruct((group, factors // group, nobl), bf16),
+            jax.ShapeDtypeStruct((factors, nsc), bf16),
+        ),
+        in_specs=[vmem] * 2,
+        out_specs=(vmem, vmem),
+        scratch_shapes=[dma((GATHER_SENDS,)), dma((2,)), dma((far_x, 2)), dma((group, 2))],
+        compiler_params=pltpu.CompilerParams(collective_id=0, has_side_effects=True),
+    )(loadings.T, scenarios)
+    loss, cont = pl.pallas_call(
         scenario_losses,
         name="scenario_losses",
         out_shape=(
-            jax.ShapeDtypeStruct((cols, LANES), f32),
+            jax.ShapeDtypeStruct((cols + TILE, LANES), f32),
             jax.ShapeDtypeStruct((rows, LANES), f32),
         ),
         in_specs=[pl.BlockSpec(memory_space=pltpu.SMEM)] + [vmem] * 6,
         out_specs=(vmem, vmem),
         scratch_shapes=[
-            pltpu.VMEM((nsc, factors), jnp.bfloat16),
-            pltpu.VMEM((nsc, LANES), f32),
-            pltpu.VMEM((nsc, LANES), f32),
-            pltpu.VMEM((8, nobl), f32),
-            pltpu.VMEM((rows, LANES), f32),
-            pltpu.VMEM((rows, LANES), f32),
-            pltpu.VMEM((rows, LANES), f32),
-            pltpu.VMEM((rows, LANES), f32),
-            pltpu.VMEM((ROWS, COLS), f32),
-            pltpu.VMEM((ROWS, COLS), f32),
+            pltpu.VMEM((factors, nobl), bf16),
+            pltpu.VMEM((nsc, factors), bf16),
+            wide(nsc, LANES), wide(nsc, LANES), wide(8, nobl),
+            wide(rows, LANES), wide(rows, LANES), wide(rows, LANES), wide(rows, LANES),
+            wide(ROWS, COLS), wide(ROWS, COLS),
         ],
     )(
-        thresholds, lt, s, rho.reshape(rows, LANES), exposure.reshape(rows, LANES),
-        rating.reshape(rows, LANES), weight.reshape(cols, LANES),
+        thresholds, lt3, panel, rho.reshape(rows, LANES), exposure.reshape(rows, LANES),
+        rating.reshape(rows, LANES), weight,
     )
-
-
-def local(loadings, scenarios, rho, exposure, rating, thresholds, tail_weight):
-    panel = lax.all_gather(scenarios, "obl", axis=0, tiled=True)
-    lt = lax.all_gather(loadings.T, "scen", axis=0, tiled=True)
-    count = loadings.shape[0] * lax.axis_size("obl")
-    loss, cont = compute(lt, panel, rho, exposure, rating, thresholds, tail_weight)
-    weights = tail_weight.astype(jnp.float32)
-    losses = lax.psum(loss.reshape(-1), "obl") / count
-    numer, total = lax.psum((cont.reshape(-1), jnp.sum(weights)), "scen")
-    contributions = numer / total
-    shortfall = lax.psum(jnp.sum(contributions), "obl") / count
-    return (losses, contributions, shortfall)
+    losses, contributions, shortfall = pl.pallas_call(
+        functools.partial(reduce, count),
+        name="reduce",
+        out_shape=(
+            jax.ShapeDtypeStruct((cols, LANES), f32),
+            jax.ShapeDtypeStruct((rows, LANES), f32),
+            jax.ShapeDtypeStruct((TILE, LANES), f32),
+        ),
+        in_specs=[vmem] * 3,
+        out_specs=(vmem, vmem, vmem),
+        scratch_shapes=[
+            wide(cols + TILE, LANES), wide(X, cols + TILE, LANES),
+            wide(rows, LANES), wide(Z, rows, LANES), wide(Y, rows, LANES), wide(group, TILE, LANES),
+            dma((REDUCE_SENDS,)), dma((2,)), dma((X,)), dma((Z,)), dma((Y,)), dma((group,)),
+        ],
+        compiler_params=pltpu.CompilerParams(collective_id=1, has_side_effects=True),
+    )(loss, cont, weight)
+    return losses.reshape(-1), contributions.reshape(-1), shortfall[0, 0]
 
 
 def solution(mesh):

time: 429 us -> 153 us (0.36)
  the two profiles are of different devices: /device:TPU:0 before, /device:TPU:1 now
where the time goes in v2:
time: 153 us
  Pallas kernels  148 us (97%)
  local copies, waits for them, and re-layouts  3.84 us (3%)
    pallas_call x1, Pallas kernels, local(): pl.pallas_call(scenario_losses, name='scenario_losses', out_shape=(jax.Sh...  82.3 us
    pallas_call x1, Pallas kernels, local(): pl.pallas_call(gather, name='gather', out_shape=(jax.ShapeDtypeStruct((gr...  41.8 us
    pallas_call x1, Pallas kernels, local(): pl.pallas_call(functools.partial(reduce, count), name='reduce', out_shape...  24.3 us

profile of v2, /device:TPU:1, one launch (start us, length us, event | category | flops | bytes accessed | tf_op | source)
XLA Modules:
  0.0 152.8 jit_solution(17540452802268394838)
XLA Ops:
  0.6 41.8 %gather.1 = (bf16[32,8,4096]{2,1,0:T(8,128)(2,1)}, bf16[256,4096]{1,0:T(8,128)(2,1)}) custom-call(bf16[8,4096]{1,0:T(8,128)(2,1)} %bitcast.10, bf16[32,4096]{1,0:T(8,128)(2,1)} %scenarios.1), custom_call_target="tpu_custom_call" | custom-call | tf_op jit(solution)/shard_map/gather/pallas_call | solution.py:341
  42.4 82.3 %scenario_losses.1 = (f32[40,128]{1,0:T(8,128)}, f32[32,128]{1,0:T(8,128)}) custom-call(f32[16]{0:T(128)} %thresholds.1, bf16[32,8,4096]{2,1,0:T(8,128)(2,1)} %get-tuple-element.10.lt3, bf16[256,4096]{1,0:T(8,128)(2,1)} %get-tuple-element.11.panel, f32[32,128]{1,0:T(8,128)} %bitcast.11, f32[32,128]{1,0:T(8,128)} %bitcast.12, s32[32,128]{1,0:T(8,128)} %bitcast.13, ...), custom_call_target="tpu_custom_call" | custom-call | tf_op jit(solution)/shard_map/scenario_losses/pallas_call | solution.py:353
  124.7 24.3 %reduce.1 = (f32[32,128]{1,0:T(8,128)}, f32[32,128]{1,0:T(8,128)}, f32[8,128]{1,0:T(8,128)}) custom-call(f32[40,128]{1,0:T(8,128)} %get-tuple-element.12.loss_a, f32[32,128]{1,0:T(8,128)} %get-tuple-element.13.cont_a, s32[32,128]{1,0:T(8,128)} %bitcast.9), custom_call_target="tpu_custom_call" | custom-call | tf_op jit(solution)/shard_map/reduce/pallas_call | solution.py:373
  149.0 1.2 slice.3
  150.2 1.3 copy.12
  151.5 1.3 copy.13

commit v3 on v2

--- a/solution.py
+++ b/solution.py
@@ -69,7 +69,8 @@
             copy.wait_send()
 
 
-GATHER_SENDS = 9 + 3 + 16 + 16
+PIECES = 4
+GATHER_SENDS = 3 + 4 + 4 + 8 + 3 + 9 + 16 + 8 + 8 + 4
 REDUCE_SENDS = 2 + 3 + 3 + 3 + 31
 
 
@@ -81,48 +82,61 @@
     pl.semaphore_wait(barrier, len(peers))
 
 
-def gather(loads, scenarios, lt3, panel, send_sems, local_sem, panel_sem, loads_sem):
+def gather(
+    loads, scenarios, lt3, panel, passing, send_sems, local_sem, panel_sem, loads_sem, passing_sem,
+):
     far, x, y, z, core = place()
     obl, scen = lax.axis_index("obl"), lax.axis_index("scen")
     height, nsc = scenarios.shape
     nobl = loads.shape[1]
-    half_h, half_w = height // 2, nobl // 2
+    width, half_w = nsc // PIECES, nobl // 2
     right, left = (x + 1) % X, (x + X - 1) % X
     up, down = (y + 1) % Y, (y + Y - 1) % Y
+
+    def along(step):
+        other = (far * Z + z + step) % (2 * Z)
+        return obl_at(other // Z, x), scen_at(y, other % Z, core)
+
+    ways = [along(2), along(2 * Z - 2)]
     meet(
         [(obl_at(1 - far, x), scen), (obl_at(far, left), scen), (obl_at(far, right), scen)]
         + [(obl, scen_at(to, z, core)) for to in (up, down)]
         + [(obl, scen_at(y, (z + k) % Z, core)) for k in range(1, Z)]
         + [(obl, scen_at(y, z, 1 - core))]
+        + ways
     )
     links = Links(send_sems)
 
-    def rows(owner, start=0, size=height):
-        return panel.at[pl.ds(pl.multiple_of(owner * height + start, half_h), size), :]
-
-    own_rows = pltpu.make_async_copy(scenarios, rows(obl), local_sem.at[0])
+    def columns(c):
+        return slice(c * width, (c + 1) * width)
+
+    def piece(owner, c):
+        return panel.at[pl.ds(pl.multiple_of(owner * height, height), height), columns(c)]
+
+    own_rows = pltpu.make_async_copy(
+        scenarios, panel.at[pl.ds(pl.multiple_of(obl * height, height), height), :], local_sem.at[0])
     own_loads = pltpu.make_async_copy(loads, lt3.at[scen], local_sem.at[1])
     own_rows.start()
     own_loads.start()
 
-    def panel_out(source, owner):
+    def panel_out(source, owner, c):
         for to in (right, left):
-            links.send(source, rows(owner), panel_sem.at[owner, 0], obl_at(far, to), scen)
-
-    def panel_relay(row):
-        low, high = obl_at(row, left), obl_at(row, right)
-        links.receive(rows(low), panel_sem.at[low, 0])
+            links.send(source, piece(owner, c), panel_sem.at[owner, c], obl_at(far, to), scen)
+
+    def panel_relay(row, c):
+        owner = obl_at(row, right if c % 2 else left)
+        links.receive(piece(owner, c), panel_sem.at[owner, c])
         links.send(
-            rows(low, 0, half_h), rows(low, 0, half_h), panel_sem.at[low, 0], obl_at(far, right), scen)
-        links.receive(rows(high), panel_sem.at[high, 0])
-        links.send(
-            rows(high, half_h, half_h), rows(high, half_h, half_h), panel_sem.at[high, 1],
-            obl_at(far, left), scen)
+            piece(owner, c), piece(owner, c), panel_sem.at[owner, c],
+            obl_at(far, left if c % 2 else right), scen)
 
     def panel_last(row):
+        for c in range(PIECES):
+            owner = obl_at(row, left if c % 2 else right)
+            links.receive(piece(owner, c), panel_sem.at[owner, c])
         across = obl_at(row, (x + 2) % X)
-        links.receive(rows(across, 0, half_h), panel_sem.at[across, 0])
-        links.receive(rows(across, half_h, half_h), panel_sem.at[across, 1])
+        for c in range(PIECES):
+            links.receive(piece(across, c), panel_sem.at[across, c])
 
     def strip(owner, part=None):
         if part is None:
@@ -155,23 +169,32 @@
     runs = [(z + k) % Z for k in range(Z)]
     for run in runs[1:]:
         links.send(loads, strip(scen), loads_sem.at[scen, 0], obl, scen_at(y, run, core))
-    links.send(scenarios, rows(obl), panel_sem.at[obl, 0], obl_at(1 - far, x), scen)
-    panel_out(scenarios, obl)
+    for c in range(PIECES):
+        links.send(scenarios.at[:, columns(c)], passing.at[c], passing_sem.at[c], *ways[c % 2])
+    for c in range(PIECES):
+        panel_out(scenarios.at[:, columns(c)], obl, c)
     loads_out(loads, scen)
     for run in runs[1:]:
         owner = scen_at(y, run, core)
         links.receive(strip(owner), loads_sem.at[owner, 0])
         loads_out(strip(owner), owner)
+    other = obl_at(1 - far, x)
+    for c in range(PIECES):
+        links.receive(passing.at[c], passing_sem.at[c])
+        origin = ways[1 - c % 2][0]
+        links.send(passing.at[c], piece(origin, c), panel_sem.at[origin, c], *ways[c % 2])
     loads_relay(runs[0])
-    panel_relay(far)
-    other = obl_at(1 - far, x)
-    links.receive(rows(other), panel_sem.at[other, 0])
-    panel_out(rows(other), other)
-    for run in runs[1:]:
-        loads_relay(run)
+    for c in range(PIECES):
+        panel_relay(far, c)
+    for c in range(PIECES):
+        links.receive(piece(other, c), panel_sem.at[other, c])
+        panel_out(piece(other, c), other, c)
+        if c > 0:
+            loads_relay(runs[c])
     for run in runs:
         loads_last(run)
-    panel_relay(1 - far)
+    for c in range(PIECES):
+        panel_relay(1 - far, c)
     for run in range(Z):
         for k in range(Y):
             owner = scen_at(k, run, 1 - core)
@@ -184,7 +207,7 @@
 
 
 def reduce(
-    count, loss_a, cont_a, weight, losses_out, cont_out, short_out,
+    loss_a, cont_a, weight, losses_out, cont_out, scalars_out,
     loss_z, loss_x, cont_c, cont_z, cont_y, tiles,
     send_sems, sums_sem, loss_sem, run_sem, y_sem, tile_sem,
 ):
@@ -219,7 +242,7 @@
     for k in range(1, X):
         links.receive(loss_x.at[(x + k) % X], loss_sem.at[(x + k) % X])
     whole = loss_x[0] + loss_x[1] + loss_x[2] + loss_x[3]
-    losses_out[...] = whole[:nrows] / count
+    losses_out[...] = whole[:nrows]
     upper = lax.broadcasted_iota(jnp.int32, (TILE, LANES), 0) < TILE // 2
     tiles[scen] = jnp.where(upper, whole[nrows:], jnp.broadcast_to(weight_sum, (TILE, LANES)))
     for k in range(1, group):
@@ -229,11 +252,16 @@
     numer = cont_y[0] + cont_y[1] + cont_y[2] + cont_y[3]
     for k in range(1, group):
         links.receive(tiles.at[(scen + k) % group], tile_sem.at[(scen + k) % group])
-    scalars = jnp.sum(tiles[...], axis=0)
+    cont_out[...] = numer
+    scalars_out[...] = jnp.sum(tiles[...], axis=0)
+    links.finish()
+
+
+def finish(count, loss, numer, scalars, losses_out, cont_out, short_out):
     total = scalars[TILE - 1 : TILE, :]
-    cont_out[...] = numer / total
-    short_out[...] = jnp.broadcast_to(scalars[0:1, :] / total / count, (TILE, LANES))
-    links.finish()
+    losses_out[...] = loss[...] / count
+    cont_out[...] = numer[...] / total
+    short_out[0, 0] = (scalars[0:1, :] / total / count)[0, 0]
 
 
 def scenario_losses(
@@ -347,7 +375,10 @@
         ),
         in_specs=[vmem] * 2,
         out_specs=(vmem, vmem),
-        scratch_shapes=[dma((GATHER_SENDS,)), dma((2,)), dma((far_x, 2)), dma((group, 2))],
+        scratch_shapes=[
+            pltpu.VMEM((PIECES, scenarios.shape[0], nsc // PIECES), bf16),
+            dma((GATHER_SENDS,)), dma((2,)), dma((far_x, PIECES)), dma((group, 2)), dma((PIECES,)),
+        ],
         compiler_params=pltpu.CompilerParams(collective_id=0, has_side_effects=True),
     )(loadings.T, scenarios)
     loss, cont = pl.pallas_call(
@@ -371,7 +402,7 @@
         rating.reshape(rows, LANES), weight,
     )
     losses, contributions, shortfall = pl.pallas_call(
-        functools.partial(reduce, count),
+        reduce,
         name="reduce",
         out_shape=(
             jax.ShapeDtypeStruct((cols, LANES), f32),
@@ -387,7 +418,18 @@
         ],
         compiler_params=pltpu.CompilerParams(collective_id=1, has_side_effects=True),
     )(loss, cont, weight)
-    return losses.reshape(-1), contributions.reshape(-1), shortfall[0, 0]
+    losses, contributions, shortfall = pl.pallas_call(
+        functools.partial(finish, count),
+        name="finish",
+        out_shape=(
+            jax.ShapeDtypeStruct((cols, LANES), f32),
+            jax.ShapeDtypeStruct((rows, LANES), f32),
+            jax.ShapeDtypeStruct((1, 1), f32),
+        ),
+        in_specs=[vmem] * 3,
+        out_specs=(vmem, vmem, pl.BlockSpec(memory_space=pltpu.SMEM)),
+    )(losses, contributions, shortfall)
+    return losses.reshape(-1), contributions.reshape(-1), shortfall.reshape(())
 
 
 def solution(mesh):

time: 153 us -> 149 us (0.974)
  local copies, waits for them, and re-layouts: 3.84 us -> 0 us
    unnamed x2 -> x0, local copies, waits for them, and re-layouts: 2.65 us -> none
    pallas_call x1 -> x2, Pallas kernels: 24.3 us -> 24.7 us  [the longest x1 23.4 us: local(): pl.pallas_call(reduce, name='reduce', out_shape=(jax.ShapeDtypeStruct((co...]
where the time goes in v3:
time: 149 us
  Pallas kernels  148 us (99%)
    pallas_call x1, Pallas kernels, local(): pl.pallas_call(scenario_losses, name='scenario_losses', out_shape=(jax.Sh...  82.3 us
    pallas_call x1, Pallas kernels, local(): pl.pallas_call(gather, name='gather', out_shape=(jax.ShapeDtypeStruct((gr...  41.3 us
    pallas_call x1, Pallas kernels, local(): pl.pallas_call(reduce, name='reduce', out_shape=(jax.ShapeDtypeStruct((co...  23.4 us

profile of v3, /device:TPU:1, one launch (start us, length us, event | category | flops | bytes accessed | tf_op | source)
XLA Modules:
  0.0 148.9 jit_solution(7794721433571629201)
XLA Ops:
  0.6 41.3 %gather.1 = (bf16[32,8,4096]{2,1,0:T(8,128)(2,1)}, bf16[256,4096]{1,0:T(8,128)(2,1)}) custom-call(bf16[8,4096]{1,0:T(8,128)(2,1)} %bitcast.10, bf16[32,4096]{1,0:T(8,128)(2,1)} %scenarios.1), custom_call_target="tpu_custom_call" | custom-call | tf_op jit(solution)/shard_map/gather/pallas_call | solution.py:369
  41.9 82.3 %scenario_losses.1 = (f32[40,128]{1,0:T(8,128)}, f32[32,128]{1,0:T(8,128)}) custom-call(f32[16]{0:T(128)} %thresholds.1, bf16[32,8,4096]{2,1,0:T(8,128)(2,1)} %get-tuple-element.13.lt3, bf16[256,4096]{1,0:T(8,128)(2,1)} %get-tuple-element.14.panel, f32[32,128]{1,0:T(8,128)} %bitcast.11, f32[32,128]{1,0:T(8,128)} %bitcast.12, s32[32,128]{1,0:T(8,128)} %bitcast.13, ...), custom_call_target="tpu_custom_call" | custom-call | tf_op jit(solution)/shard_map/scenario_losses/pallas_call | solution.py:384
  124.1 23.4 %reduce.1 = (f32[32,128]{1,0:T(8,128)}, f32[32,128]{1,0:T(8,128)}, f32[8,128]{1,0:T(8,128)}) custom-call(f32[40,128]{1,0:T(8,128)} %get-tuple-element.15.loss_a, f32[32,128]{1,0:T(8,128)} %get-tuple-element.16.cont_a, s32[32,128]{1,0:T(8,128)} %bitcast.9), custom_call_target="tpu_custom_call" | custom-call | tf_op jit(solution)/shard_map/reduce/pallas_call | solution.py:404
  147.5 1.4 finish.1

commit v4 on v3

--- a/solution.py
+++ b/solution.py
@@ -9,7 +9,7 @@
 from jax.sharding import PartitionSpec as P
 
 LANES = 128
-ROWS = 256
+ROWS = 512
 COLS = 512
 
 SCALE = float(2.0**-3.4)
@@ -99,7 +99,7 @@
 
     ways = [along(2), along(2 * Z - 2)]
     meet(
-        [(obl_at(1 - far, x), scen), (obl_at(far, left), scen), (obl_at(far, right), scen)]
+        [(obl_at(far, left), scen), (obl_at(far, right), scen)]
         + [(obl, scen_at(to, z, core)) for to in (up, down)]
         + [(obl, scen_at(y, (z + k) % Z, core)) for k in range(1, Z)]
         + [(obl, scen_at(y, z, 1 - core))]
@@ -190,11 +190,11 @@
         links.receive(piece(other, c), panel_sem.at[other, c])
         panel_out(piece(other, c), other, c)
         if c > 0:
+            panel_relay(1 - far, c - 1)
             loads_relay(runs[c])
+    panel_relay(1 - far, PIECES - 1)
     for run in runs:
         loads_last(run)
-    for c in range(PIECES):
-        panel_relay(1 - far, c)
     for run in range(Z):
         for k in range(Y):
             owner = scen_at(k, run, 1 - core)

time: 149 us -> 144 us (0.966)
  Pallas kernels: 148 us -> 143 us
    pallas_call x1, Pallas kernels: 82.3 us -> 75.7 us  [local(): pl.pallas_call(scenario_losses, name='scenario_losses', out_shape=(jax.Sh...]
    pallas_call x1, Pallas kernels: 41.3 us -> 45.4 us  [local(): pl.pallas_call(gather, name='gather', out_shape=(jax.ShapeDtypeStruct((gr...]
    pallas_call x1, Pallas kernels: 23.4 us -> 20.1 us  [local(): pl.pallas_call(reduce, name='reduce', out_shape=(jax.ShapeDtypeStruct((co...]
where the time goes in v4:
time: 144 us; the launch traced here: 143 us
  Pallas kernels  143 us (99%)
    pallas_call x1, Pallas kernels, local(): pl.pallas_call(scenario_losses, name='scenario_losses', out_shape=(jax.Sh...  75.7 us
    pallas_call x1, Pallas kernels, local(): pl.pallas_call(gather, name='gather', out_shape=(jax.ShapeDtypeStruct((gr...  45.4 us
    pallas_call x1, Pallas kernels, local(): pl.pallas_call(reduce, name='reduce', out_shape=(jax.ShapeDtypeStruct((co...  20.1 us

profile of v4, /device:TPU:1, one launch (start us, length us, event | category | flops | bytes accessed | tf_op | source)
XLA Modules:
  0.0 143.2 jit_solution(10867201414588535430)
XLA Ops:
  0.6 45.4 %gather.1 = (bf16[32,8,4096]{2,1,0:T(8,128)(2,1)}, bf16[256,4096]{1,0:T(8,128)(2,1)}) custom-call(bf16[8,4096]{1,0:T(8,128)(2,1)} %bitcast.10, bf16[32,4096]{1,0:T(8,128)(2,1)} %scenarios.1), custom_call_target="tpu_custom_call" | custom-call | tf_op jit(solution)/shard_map/gather/pallas_call | solution.py:369
  46.0 75.7 %scenario_losses.1 = (f32[40,128]{1,0:T(8,128)}, f32[32,128]{1,0:T(8,128)}) custom-call(f32[16]{0:T(128)} %thresholds.1, bf16[32,8,4096]{2,1,0:T(8,128)(2,1)} %get-tuple-element.13.lt3, bf16[256,4096]{1,0:T(8,128)(2,1)} %get-tuple-element.14.panel, f32[32,128]{1,0:T(8,128)} %bitcast.11, f32[32,128]{1,0:T(8,128)} %bitcast.12, s32[32,128]{1,0:T(8,128)} %bitcast.13, ...), custom_call_target="tpu_custom_call" | custom-call | tf_op jit(solution)/shard_map/scenario_losses/pallas_call | solution.py:384
  121.8 20.1 %reduce.1 = (f32[32,128]{1,0:T(8,128)}, f32[32,128]{1,0:T(8,128)}, f32[8,128]{1,0:T(8,128)}) custom-call(f32[40,128]{1,0:T(8,128)} %get-tuple-element.15.loss_a, f32[32,128]{1,0:T(8,128)} %get-tuple-element.16.cont_a, s32[32,128]{1,0:T(8,128)} %bitcast.9), custom_call_target="tpu_custom_call" | custom-call | tf_op jit(solution)/shard_map/reduce/pallas_call | solution.py:404
  141.8 1.4 finish.1

commit v5 on v4

--- a/solution.py
+++ b/solution.py
@@ -9,7 +9,7 @@
 from jax.sharding import PartitionSpec as P
 
 LANES = 128
-ROWS = 512
+ROWS = 1024
 COLS = 512
 
 SCALE = float(2.0**-3.4)
@@ -183,14 +183,15 @@
         links.receive(passing.at[c], passing_sem.at[c])
         origin = ways[1 - c % 2][0]
         links.send(passing.at[c], piece(origin, c), panel_sem.at[origin, c], *ways[c % 2])
-    loads_relay(runs[0])
-    for c in range(PIECES):
         panel_relay(far, c)
+        if c == 0:
+            loads_relay(runs[0])
     for c in range(PIECES):
         links.receive(piece(other, c), panel_sem.at[other, c])
         panel_out(piece(other, c), other, c)
         if c > 0:
             panel_relay(1 - far, c - 1)
+        if 0 < c < Z:
             loads_relay(runs[c])
     panel_relay(1 - far, PIECES - 1)
     for run in runs:

time: 144 us -> 140 us (0.972)
  Pallas kernels: 143 us -> 139 us
    pallas_call x1, Pallas kernels: 75.7 us -> 72.7 us  [local(): pl.pallas_call(scenario_losses, name='scenario_losses', out_shape=(jax.Sh...]
    pallas_call x1, Pallas kernels: 45.4 us -> 43.9 us  [local(): pl.pallas_call(gather, name='gather', out_shape=(jax.ShapeDtypeStruct((gr...]
where the time goes in v5:
time: 140 us
  Pallas kernels  139 us (99%)
    pallas_call x1, Pallas kernels, local(): pl.pallas_call(scenario_losses, name='scenario_losses', out_shape=(jax.Sh...  72.7 us
    pallas_call x1, Pallas kernels, local(): pl.pallas_call(gather, name='gather', out_shape=(jax.ShapeDtypeStruct((gr...  43.9 us
    pallas_call x1, Pallas kernels, local(): pl.pallas_call(reduce, name='reduce', out_shape=(jax.ShapeDtypeStruct((co...  21.4 us

profile of v5, /device:TPU:1, one launch (start us, length us, event | category | flops | bytes accessed | tf_op | source)
XLA Modules:
  0.0 140.0 jit_solution(11681147156530698020)
XLA Ops:
  0.6 43.9 %gather.1 = (bf16[32,8,4096]{2,1,0:T(8,128)(2,1)}, bf16[256,4096]{1,0:T(8,128)(2,1)}) custom-call(bf16[8,4096]{1,0:T(8,128)(2,1)} %bitcast.10, bf16[32,4096]{1,0:T(8,128)(2,1)} %scenarios.1), custom_call_target="tpu_custom_call" | custom-call | tf_op jit(solution)/shard_map/gather/pallas_call | solution.py:370
  44.5 72.7 %scenario_losses.1 = (f32[40,128]{1,0:T(8,128)}, f32[32,128]{1,0:T(8,128)}) custom-call(f32[16]{0:T(128)} %thresholds.1, bf16[32,8,4096]{2,1,0:T(8,128)(2,1)} %get-tuple-element.13.lt3, bf16[256,4096]{1,0:T(8,128)(2,1)} %get-tuple-element.14.panel, f32[32,128]{1,0:T(8,128)} %bitcast.11, f32[32,128]{1,0:T(8,128)} %bitcast.12, s32[32,128]{1,0:T(8,128)} %bitcast.13, ...), custom_call_target="tpu_custom_call" | custom-call | tf_op jit(solution)/shard_map/scenario_losses/pallas_call | solution.py:385
  117.2 21.4 %reduce.1 = (f32[32,128]{1,0:T(8,128)}, f32[32,128]{1,0:T(8,128)}, f32[8,128]{1,0:T(8,128)}) custom-call(f32[40,128]{1,0:T(8,128)} %get-tuple-element.15.loss_a, f32[32,128]{1,0:T(8,128)} %get-tuple-element.16.cont_a, s32[32,128]{1,0:T(8,128)} %bitcast.9), custom_call_target="tpu_custom_call" | custom-call | tf_op jit(solution)/shard_map/reduce/pallas_call | solution.py:405
  138.7 1.4 finish.1
